TPU v7x, 256 devices: a whole 4x4x8 slice. The times are simulated.
256 devices in a mesh: loop: 32 (over z, x_lo, core), group: 8 (over y, x_hi).
Axes of the slice: x: 4 (x_hi: 2, x_lo: 2; x = x_hi * 2 + x_lo), y: 4, z: 8, core: 2. Of those that a mesh axis runs over, the one named last changes fastest.
Arguments:
- images: bfloat16 [8, 256, 7, 7, 1536], P('group', 'loop'), as said below
- targets: int32 [8, 256], P('group'), may hold values from 0 to 131071, as said below
- kernel: bfloat16 [7, 7, 1536], replicated, may hold values from -0.875 to 0.875
- projection: bfloat16 [1536, 768], replicated, as said below
- captions: bfloat16 [131072, 768], P('loop'), as said below
Outputs:
- loss: float32 [8, 256], P('group', 'loop')
- image_grad: bfloat16 [8, 256, 7, 7, 1536], P('group', 'loop')
- kernel_grad: float32 [1536, 49], P(('loop', 'group'))
Inputs may be any that keep to these rules, and one draw needn't show every extreme that they name: targets index captions of the whole gallery. `images`: finite real values. `projection`: finite real values. `captions`: finite real values, no caption all zero.
All inputs are finite; a program needn't handle non-finite values.
Results may differ from a plain program's by a relative error of at most 0.0066.
Values may be sent and summed in bfloat16 or wider, within the bound.
A program may use at most 64 MiB of HBM per device.

v0:
```python
import jax
import jax.numpy as jnp
from jax import lax
from jax.sharding import PartitionSpec as P

logit_sharpness = 20.0


def depthwise(padded, kernel):
    reach = kernel.shape[0]
    side = padded.shape[1] - reach + 1
    total = jnp.zeros((padded.shape[0], side, side, padded.shape[3]), jnp.float32)
    for row_off in range(reach):
        for col_off in range(reach):
            window = padded[:, row_off : row_off + side, col_off : col_off + side, :].astype(
                jnp.float32
            )
            total = total + window * kernel[row_off, col_off].astype(jnp.float32)
    return total


def forward(pixels, kernel, projection):
    margin = kernel.shape[0] // 2
    padded = jnp.pad(pixels, ((0, 0), (margin, margin), (margin, margin), (0, 0)))
    hidden = depthwise(padded, kernel)
    centre = hidden - jnp.mean(hidden, -1, keepdims=True)
    scale_inv = lax.rsqrt(jnp.mean(centre * centre, -1, keepdims=True) + 1e-06)
    normed = centre * scale_inv
    pooled = jnp.mean(pixels.astype(jnp.float32) + normed, axis=(1, 2)).astype(jnp.bfloat16)
    embedded = jnp.dot(pooled, projection, preferred_element_type=jnp.float32)
    inv_norm = lax.rsqrt(jnp.sum(embedded * embedded, -1, keepdims=True) + 1e-06)
    return (padded, normed, scale_inv, embedded, inv_norm)


def backward(padded, normed, scale_inv, embedded, inv_norm, kernel, projection, query_gradient):
    unit = embedded * inv_norm
    emb_grad = (
        (query_gradient - unit * jnp.sum(unit * query_gradient, -1, keepdims=True)) * inv_norm
    ).astype(jnp.bfloat16)
    pooled_grad = lax.dot_general(
        emb_grad, projection, (((1,), (1,)), ((), ())), preferred_element_type=jnp.float32
    )
    side = normed.shape[1]
    out_grad = (pooled_grad / (side * side))[:, None, None, :]
    hidden_grad = scale_inv * (
        out_grad
        - jnp.mean(out_grad, -1, keepdims=True)
        - normed * jnp.mean(normed * out_grad, -1, keepdims=True)
    )
    reach = kernel.shape[0]
    margin = reach // 2
    grad_pad = jnp.pad(hidden_grad, ((0, 0), (margin, margin), (margin, margin), (0, 0)))
    input_grad = out_grad + depthwise(grad_pad, kernel[::-1, ::-1])
    taps = []
    for row_off in range(reach):
        for col_off in range(reach):
            window = padded[:, row_off : row_off + side, col_off : col_off + side, :].astype(
                jnp.float32
            )
            taps.append(jnp.sum(window * hidden_grad, axis=(0, 1, 2)))
    return (input_grad, jnp.stack(taps, 0).T)


def normalize(captions):
    values = captions.astype(jnp.float32)
    return (values * lax.rsqrt(jnp.sum(values * values, -1, keepdims=True) + 1e-06)).astype(
        jnp.bfloat16
    )


def shards(images, targets, kernel, projection, captions):
    pixels = images[0]
    group_targets = targets[0]
    own_rows = pixels.shape[0]
    cap_rows = captions.shape[0]
    group_rows = group_targets.shape[0]
    padded, normed, scale_inv, embedded, inv_norm = forward(pixels, kernel, projection)
    query = (embedded * inv_norm).astype(jnp.bfloat16)
    normalized_caption_vectors = normalize(captions)
    similarity_scores = logit_sharpness * lax.dot_general(
        lax.all_gather(query, "loop", axis=0, tiled=True),
        normalized_caption_vectors,
        (((1,), (1,)), ((), ())),
        preferred_element_type=jnp.float32,
    )
    col_part = jnp.sum(jnp.exp(similarity_scores), 0)
    col_log = jnp.log(lax.psum(col_part, "group"))
    weight = jnp.exp(similarity_scores - col_log)
    local_index = group_targets - lax.axis_index("loop") * cap_rows
    onehot = (
        local_index[:, None] == lax.broadcasted_iota(jnp.int32, (group_rows, cap_rows), 1)
    ).astype(jnp.float32)
    row_part = jnp.sum(weight, 1)
    target_part = jnp.sum(onehot * (similarity_scores - col_log), 1)
    row_sum, target_logit = lax.psum((row_part, target_part), "loop")
    loss_group = jnp.log(row_sum) - target_logit
    own_start = lax.axis_index("loop") * own_rows
    own_loss = lax.dynamic_slice_in_dim(loss_group, own_start, own_rows, 0)
    grad = weight / row_sum[:, None] - onehot
    col_grad = lax.psum(jnp.sum(grad, 0), "group")
    similarity_gradient = (grad - weight * col_grad).astype(jnp.bfloat16)
    incomplete_gradient = logit_sharpness * jnp.dot(
        similarity_gradient, normalized_caption_vectors, preferred_element_type=jnp.float32
    )
    summed = lax.psum(incomplete_gradient, "loop")
    query_gradient = lax.dynamic_slice_in_dim(summed, own_start, own_rows, 0)
    input_grad, kernel_terms = backward(
        padded, normed, scale_inv, embedded, inv_norm, kernel, projection, query_gradient
    )
    kernel_share = lax.psum_scatter(
        kernel_terms, ("loop", "group"), scatter_dimension=0, tiled=True
    )
    return (own_loss[None], input_grad.astype(jnp.bfloat16)[None], kernel_share)


def solution(mesh):
    placed = (P("group", "loop", None, None, None), P("group", None), P(), P(), P("loop", None))
    return jax.shard_map(
        shards,
        mesh=mesh,
        in_specs=placed,
        out_specs=(
            P("group", "loop"),
            P("group", "loop", None, None, None),
            P(("loop", "group"), None),
        ),
        check_vma=False,
    )
```

profile of v0, /device:TPU:1, one launch (start us, length us, event | category | flops | bytes accessed | tf_op | source)
XLA Modules:
  0.0 739.3 jit_solution(11930092785954452918)
XLA Ops:
  7.2 0.0 copy-start
  7.2 0.0 all-reduce.6.cloned.1.call-start
  7.2 1.2 convert_reduce_fusion.46
  8.5 1.5 convert_reduce_fusion.48
  10.0 1.6 convert_reduce_fusion.47
  11.6 0.0 copy-start.3
  11.6 31.9 %fusion.216 = (f32[8,7,7]{0,2,1:T(8,128)S(1)}, f32[8,7,7,1536]{3,0,2,1:T(8,128)S(1)}) fusion(f32[1536]{0:T(1024)S(1)} %get-tuple-element.107, f32[1536]{0:T(1024)S(1)} %get-tuple-element.108, f32[1536]{0:T(1024)S(1)} %get-tuple-element.61, f32[1536]{0:T(1024)S(1)} %get-tuple-element.62, f32[1536]{0:T(1024)S(1)} %get-tuple-element.63, ...), kind=kLoop, calls=%fused_computation.486 | loop fusion | flops 88510072 | bytes 3915296 | tf_op jit(solution)/shard_map/reduce_sum | solution.py:26
  43.5 0.0 copy-start.1
  43.5 0.4 multiply_reduce_fusion.1
  43.9 0.0 copy-done.3
  43.9 0.0 copy-start.6
  43.9 0.5 fusion.103
  44.4 0.5 copy-done.1
  44.9 0.0 copy-done
  44.9 0.5 multiply_reduce_fusion.3
  45.5 0.1 multiply_convert_fusion.3
  45.6 39.6 %all_gather.3 = bf16[256,768]{1,0:T(8,128)(2,1)S(1)} all-gather(bf16[8,768]{1,0:T(8,128)(2,1)S(1)} %multiply_convert_fusion.3), channel_id=1, replica_groups=mesh['loop'=32,'group'=8] {'loop'}, dimensions={0}, use_global_device_ids=true | all-gather | bytes 405504 | tf_op jit(solution)/shard_map/all_gather | solution.py:81
  85.2 0.0 copy-done.6
  85.2 1.3 fusion
  86.5 3.8 exponential_reduce_fusion
  90.4 34.7 %psum.35 = f32[4096]{0:T(1024)S(1)} all-reduce(f32[4096]{0:T(1024)S(1)} %get-tuple-element.114), channel_id=1, replica_groups=mesh['loop'=32,'group'=8] {'group'}, use_global_device_ids=true, to_apply=%region_6.7 | all-reduce | flops 4096 | bytes 32768 | tf_op jit(solution)/shard_map/psum | solution.py:87
  125.1 2.8 fusion.3
  127.9 59.8 %psum.36 = f32[256]{0:T(256)S(1)} all-reduce(f32[256]{0:T(256)S(1)} %fusion.3), channel_id=1, replica_groups=mesh['loop'=32,'group'=8] {'loop'}, use_global_device_ids=true, to_apply=%region_8.9 | all-reduce | flops 256 | bytes 2048 | tf_op jit(solution)/shard_map/psum | solution.py:95
  187.7 0.0 copy-done.7
  187.7 4.2 fusion.2
  191.9 30.1 %psum.38 = f32[4096]{0:T(1024)S(1)} all-reduce(f32[4096]{0:T(1024)S(1)} %get-tuple-element.9), channel_id=1, replica_groups=mesh['loop'=32,'group'=8] {'group'}, use_global_device_ids=true, to_apply=%region_12.13 | all-reduce | flops 4096 | bytes 32768 | tf_op jit(solution)/shard_map/psum | solution.py:100
  222.0 8.0 %fusion.206 = f32[256,768]{1,0:T(8,128)} fusion(bf16[4096,768]{1,0:T(8,128)(2,1)} %param.9, f32[4096]{0:T(1024)S(1)} %add_rsqrt_fusion.1, f32[256,4096]{1,0:T(8,128)} %get-tuple-element.115, f32[4096]{0:T(1024)S(1)} %psum.38, f32[256]{0:T(256)S(1)} %psum.36, s32[256]{0:T(256)S(1)} %bitcast.20, f32[4096]{0:T(1024)S(1)} %log.6), kind=kOutput, calls=%fused_computation.413 | convolution fusion | flops 1628635136 | bytes 11323392 | tf_op jit(solution)/shard_map/dot_general | solution.py:102
  230.0 0.0 all-reduce.6.cloned.1.call-update
  230.0 0.0 all-reduce.8.cloned.1.call-start
  230.1 59.9 %psum.37 = f32[256]{0:T(256)S(1)} all-reduce(f32[256]{0:T(256)S(1)} %get-tuple-element.10), channel_id=1, replica_groups=mesh['loop'=32,'group'=8] {'loop'}, use_global_device_ids=true, to_apply=%region_10.11 | all-reduce | flops 256 | bytes 2048 | tf_op jit(solution)/shard_map/psum | solution.py:95
  290.0 0.6 dynamic-slice_bitcast_fusion
  290.6 167.9 %all-reduce.6.cloned.1.call-done = f32[256,768]{1,0:T(8,128)} async-done(((f32[256,768]{1,0:T(8,128)}), f32[256,768]{1,0:T(8,128)}) %all-reduce.6.cloned.1.call-update) | async-done | bytes 786448 | tf_op jit(solution)/shard_map/psum | solution.py:105
  458.5 1.1 multiply_reduce_fusion.2
  459.6 1.7 fusion.218
  461.3 0.0 copy-done.2
  461.3 0.5 multiply_reduce_fusion
  461.8 0.1 broadcast_subtract_fusion
  461.8 0.0 copy-done.4
  461.8 7.7 %fusion.102 = (f32[1536]{0:T(1024)S(1)}, f32[1536]{0:T(1024)S(1)}, f32[1536]{0:T(1024)S(1)}, f32[1536]{0:T(1024)S(1)}, f32[1536]{0:T(1024)S(1)}, /*index=5*/f32[...) fusion(bf16[8,7,7,1536]{3,0,2,1:T(8,128)(2,1)S(1)} %bitcast.15,, ...), kind=kLoop, calls=%fused_computation.304 | loop fusion | flops 35496960 | bytes 6185568 | tf_op jit(solution)/shard_map/reduce_sum | solution.py:60
  469.6 0.0 copy-start.5
  469.6 2.3 fusion.43
  472.0 3.5 fusion.84
  476.2 4.8 stack.199
  480.9 0.0 all-reduce.8.cloned.1.call-update
  481.0 38.0 %fusion.209 = bf16[1,8,7,7,1536]{4,1,3,2,0:T(8,128)(2,1)} fusion(f32[1536]{0:T(1024)S(1)} %get-tuple-element.60, f32[8,7,7,1536]{3,0,2,1:T(8,128)} %copy-done.5, f32[1536]{0:T(1024)S(1)} %get-tuple-element.79, f32[1536]{0:T(1024)S(1)} %get-tuple-element.98, f32[1536]{0:T(1024)S(1)} %get-tuple-element.106, f32[1536]{0:T(1024)S(1)} %get-tuple-element.105, ...), kind=kLoop, calls=%fused_computation.414 | loop fusion | flops 59609088 | bytes 3962880 | tf_op jit(solution)/shard_map/broadcast_in_dim | solution.py:113
  519.0 211.9 %all-reduce.8.cloned.1.call-done = f32[1536,49]{0,1:T(8,128)} async-done(((f32[1536,49]{0,1:T(8,128)}), f32[1536,49]{0,1:T(8,128)}) %all-reduce.8.cloned.1.call-update) | async-done | bytes 301072
  730.9 0.9 constant_dynamic-slice_fusion
  731.7 0.7 copy.9
  (62 shorter events, 0.4 us)
Async XLA Ops:
  7.2 37.8 %copy-start = (bf16[1536,768]{1,0:T(8,128)(2,1)S(1)}, bf16[1536,768]{1,0:T(8,128)(2,1)}, u32[]{:S(2)}) copy-start(bf16[1536,768]{1,0:T(8,128)(2,1)} %param.8) | copy-start | bytes 7077892
  7.2 451.3 %all-reduce.6.cloned.1.call-start = ((), (), s32[]{:S(2)}) async-start(), calls=%async_computation | async-start | bytes 1572864 | tf_op jit(solution)/shard_map/psum | solution.py:105
  11.6 32.3 %copy-start.3 = (bf16[1,8,7,7,1536]{4,1,3,2,0:T(8,128)(2,1)S(1)}, bf16[1,8,7,7,1536]{4,1,3,2,0:T(8,128)(2,1)}, u32[]{:S(2)}) copy-start(bf16[1,8,7,7,1536]{4,1,3,2,0:T(8,128)(2,1)} %param.5) | copy-start | bytes 3612676
  43.5 1.5 copy-start.1
  43.9 41.3 %copy-start.6 = (bf16[4096,768]{1,0:T(8,128)(2,1)S(1)}, bf16[4096,768]{1,0:T(8,128)(2,1)}, u32[]{:S(2)}) copy-start(bf16[4096,768]{1,0:T(8,128)(2,1)} %param.9) | copy-start | bytes 18874372
  90.4 97.4 %copy-start.7 = (s32[1,256]{1,0:T(1,128)S(1)}, s32[1,256]{1,0:T(1,128)}, u32[]{:S(2)}) copy-start(s32[1,256]{1,0:T(1,128)} %param.6) | copy-start | bytes 3076
  230.0 500.8 %all-reduce.8.cloned.1.call-start = ((), (), s32[]{:S(2)}) async-start(), calls=%async_computation.1 | async-start | bytes 688128
  458.5 2.8 copy-start.2
  459.6 2.3 copy-start.4
  469.6 2.4 copy-start.5
Sparse Core Ops, SparseCore 0:
  230.1 228.3 all-reduce.5
  481.1 249.7 all-reduce.7
where the time goes:
time: 740 us; the launch traced here: 739 us
  waiting for transfers between devices  380 us (51%)
  blocking collectives  224 us (30%)
  other arithmetic  98.7 us (13%)
  between operations  14.6 us (2%)
  matrix products  14.1 us (2%)
  local copies, waits for them, and re-layouts  7.81 us (1%)
    unnamed x3, waiting for transfers between devices  212 us
    psum x1, waiting for transfers between devices, shards(): summed = lax.psum(incomplete_gradient, 'loop')  168 us
    psum x2, blocking collectives, shards(): row_sum, target_logit = lax.psum((row_part, target_part), 'loop')  120 us
    all_gather x1, blocking collectives, shards(): lax.all_gather(query, 'loop', axis=0, tiled=True)  39.6 us
    broadcast_in_dim x1, other arithmetic, shards(): return (own_loss[None], input_grad.astype(jnp.bfloat16)[None], kernel_share)  38 us
    psum x1, blocking collectives, shards(): col_log = jnp.log(lax.psum(col_part, 'group'))  34.7 us
    reduce_sum x1, other arithmetic, forward(): centre = hidden - jnp.mean(hidden, -1, keepdims=True)  31.9 us
    psum x1, blocking collectives, shards(): col_grad = lax.psum(jnp.sum(grad, 0), 'group')  30.1 us
  transfers between devices with their start and end apart: 2, of which 2 were waited for; matrix products, arithmetic and copies ran while one was open for 5% of the time, Pallas kernels for 0%

commit v1 on v0

v1 whole, which is shorter than its diff:
```python
import jax
import jax.numpy as jnp
from jax import lax
from jax.experimental import pallas as pl
from jax.experimental.pallas import tpu as pltpu
from jax.sharding import PartitionSpec as P

MESH = pl.DeviceIdType.MESH
f32, bf16 = jnp.float32, jnp.bfloat16

SCALE = 20.0
EPS = 1e-06
C, D, S = 1536, 768, 7
T = C // 128
PIX = S * S
L, G = 32, 8
N = 8
H = L // 2
Q = L * N
CAPS = 4096
CH = 512
NCH = CAPS // CH


def remote(src, dst, send, recv, where):
    return pltpu.make_async_remote_copy(
        src_ref=src, dst_ref=dst, send_sem=send, recv_sem=recv, device_id=where, device_id_type=MESH
    )


def hop(pos, k):
    step, low = k // 2, k % 2
    half = (step + 1) // 2
    z = (pos // 2 + 4 + half * (2 * (step % 2) - 1)) % 8
    return z * 2 + (pos + low) % 2


def conv_rows(load, tap, flip):
    for i in range(S):
        acc = [None] * S
        for a in range(S):
            r = i + a - 3
            if not 0 <= r < S:
                continue
            row = [load(r, x) for x in range(S)]
            for b in range(S):
                w = tap(S - 1 - a, S - 1 - b) if flip else tap(a, b)
                for j in range(S):
                    x = j + b - 3
                    if 0 <= x < S:
                        term = row[x] * w
                        acc[j] = term if acc[j] is None else acc[j] + term
        yield i, acc


def mega(
    img_hbm, tgt_ref, ker_ref, proj_hbm, cap_hbm,
    loss_ref, ig_ref, kg_ref,
    img, proj, u, xf, kf, tmp, nf, rsb, xs,
    qslots, qb, tcol, iot, cnt, e, irc, sgb, cols, cols2, rows,
    pacc, prec, rsend, rrec, dkr, kgt, kps, kprec, krec, krec2,
    in_sem, ag_s, ag_r, fw_s, c1_s, c1_r, c2_s, c2_r, rw_s, rw_r,
    pp_s, pp_r, rs_s, rs_r, kp_s, kp_r, ks_s, ks_r, k2_s, k2_r,
):
    me = lax.axis_index("loop")
    grp = lax.axis_index("group")
    core, pos = me % 2, me // 2
    mate = {"loop": me + 1 - 2 * core}
    slot = core * H + pos

    def peer(p):
        return {"loop": p * 2 + core}

    c_img = pltpu.make_async_copy(img_hbm, img, in_sem.at[0])
    c_proj = pltpu.make_async_copy(proj_hbm, proj, in_sem.at[1])
    c_cap = pltpu.make_async_copy(cap_hbm, u, in_sem.at[2])
    c_img.start()
    c_proj.start()
    c_cap.start()
    barrier = pltpu.get_barrier_semaphore()

    def greet_loop(k, carry):
        pl.semaphore_signal(barrier, inc=1, device_id={"loop": (me + k) % L}, device_id_type=MESH)
        return carry

    def greet_group(k, carry):
        pl.semaphore_signal(barrier, inc=1, device_id={"group": (grp + k) % G}, device_id_type=MESH)
        return carry

    lax.fori_loop(1, L, greet_loop, 0)
    lax.fori_loop(1, G, greet_group, 0)

    def lanes(t):
        return pl.ds(pl.multiple_of(t * 128, 128), 128)

    c_img.wait()

    def forward_tile(t, carry):
        for n in range(N):
            for i in range(S):
                tmp[n * 56 + i * 8 : n * 56 + i * 8 + S, :] = img[n, i, :, lanes(t)].astype(f32)
        for a in range(S):
            kf[t, a * 8 : a * 8 + S, :] = ker_ref[a, :, lanes(t)].astype(f32)
        total = None
        for i in range(S):
            for j in range(S):
                v = tmp[pl.ds(i * 8 + j, N, stride=56), :]
                xf[t, i * S + j] = v
                total = v if total is None else total + v
        xs[t] = total
        for i, acc in conv_rows(
            lambda r, x: xf[t, r * S + x],
            lambda a, b: jnp.broadcast_to(kf[t, a * 8 + b : a * 8 + b + 1, :], (N, 128)),
            False,
        ):
            for j in range(S):
                nf[t, i * S + j] = acc[j]
        return carry

    lax.fori_loop(0, T, forward_tile, 0)

    def norm_row(i, acc):
        for j in range(S):
            p = i * S + j
            h = nf[:, p]
            mu = jnp.sum(jnp.sum(h, axis=0), axis=1, keepdims=True) * (1.0 / C)
            cen = h - mu[None]
            var = jnp.sum(jnp.sum(cen * cen, axis=0), axis=1, keepdims=True) * (1.0 / C)
            rs = lax.rsqrt(var + EPS)
            rsb[p] = jnp.broadcast_to(rs, (N, 128))
            nrm = cen * rs[None]
            nf[:, p] = nrm
            acc = acc + nrm
        return acc

    nsum = lax.fori_loop(0, S, norm_row, xs[...])
    pooled = (nsum * (1.0 / PIX)).astype(bf16)
    pooled = jnp.concatenate([pooled[t] for t in range(T)], axis=1)
    c_proj.wait()
    embedded = jnp.dot(pooled, proj[...], preferred_element_type=f32)
    inv_norm = lax.rsqrt(jnp.sum(embedded * embedded, axis=1, keepdims=True) + EPS)
    unit = embedded * inv_norm
    qslots[slot] = unit.astype(bf16)

    pl.semaphore_wait(barrier, L - 1 + G - 1)
    own_q = qslots.at[slot]

    def ag_send(k, carry):
        to = hop(pos, k + k // (H - 2))
        remote(own_q, own_q, ag_s.at[k], ag_r.at[slot], peer(to)).start()
        return carry

    lax.fori_loop(0, H - 1, ag_send, 0)
    remote(own_q, own_q, fw_s.at[0], ag_r.at[slot], mate).start()

    c_cap.wait()

    def unit_rows(r, carry):
        rng = pl.ds(pl.multiple_of(r * 128, 128), 128)
        v = u[rng, :].astype(f32)
        u[rng, :] = (v * lax.rsqrt(jnp.sum(v * v, axis=1, keepdims=True) + EPS)).astype(bf16)
        return carry

    lax.fori_loop(0, CAPS // 128, unit_rows, 0)
    local = (tgt_ref[...] - me * CAPS).astype(f32)
    for h in range(2):
        col = jnp.transpose(jnp.broadcast_to(local[:, h * 128 : h * 128 + 128], (128, 128)))
        for b in range(16):
            l = h * 16 + b
            s = (l % 2) * H + l // 2
            tcol[s * N : s * N + N, :] = col[b * N : b * N + N, :]
    iot[...] = lax.broadcasted_iota(jnp.int32, (N, CH), 1).astype(f32)

    def wide(x):
        return jnp.concatenate([x] * (CH // 128), axis=1)

    def hits(r, rng):
        ids = iot[0:1, :] + (r * CH).astype(f32)
        return wide(tcol[rng, :]) == ids

    def count(r, carry):
        cnt[pl.ds(r, 1), :] = jnp.sum(jnp.where(hits(r, slice(None)), 1.0, 0.0), axis=0, keepdims=True)
        return carry

    lax.fori_loop(0, NCH, count, 0)

    def ag_forward(k, carry):
        frm = core * H + (pos + k) % H
        got = qslots.at[frm]
        remote(got, got, ag_s.at[0], ag_r.at[frm], mate).wait_recv()
        remote(got, got, fw_s.at[k], ag_r.at[frm], mate).start()
        return carry

    lax.fori_loop(1, H, ag_forward, 0)

    def ag_mate(k, carry):
        frm = (1 - core) * H + k
        got = qslots.at[frm]
        remote(got, got, ag_s.at[0], ag_r.at[frm], mate).wait_recv()
        return carry

    lax.fori_loop(0, H, ag_mate, 0)

    def ag_done(k, carry):
        remote(own_q, own_q, ag_s.at[k], ag_r.at[0], mate).wait_send()
        return carry

    def fw_done(k, carry):
        remote(own_q, own_q, fw_s.at[k], ag_r.at[0], mate).wait_send()
        return carry

    qb[...] = qslots[...].astype(f32).reshape(Q, D).astype(bf16)

    def scores(r, carry):
        rng = pl.ds(pl.multiple_of(r * CH, CH), CH)
        s = lax.dot_general(qb[...], u[rng, :], (((1,), (1,)), ((), ())), preferred_element_type=f32)
        v = jnp.exp(SCALE * s)
        e[r] = v
        cols[grp, pl.ds(r, 1), :] = jnp.sum(v, axis=0, keepdims=True)
        return carry

    lax.fori_loop(0, NCH, scores, 0)
    lax.fori_loop(0, H - 1, ag_done, 0)
    lax.fori_loop(0, H, fw_done, 0)

    def group_exchange(buf, send, recv):
        own = buf.at[grp]

        def start(k, carry):
            remote(own, own, send.at[k], recv.at[grp], {"group": (grp + k) % G}).start()
            return carry

        def arrive(k, carry):
            frm = (grp + k) % G
            remote(own, buf.at[frm], send.at[k], recv.at[frm], {"group": frm}).wait()
            return carry

        lax.fori_loop(1, G, start, 0)
        return lambda: lax.fori_loop(1, G, arrive, 0)

    group_exchange(cols, c1_s, c1_r)()
    ic = 1.0 / jnp.sum(cols[...], axis=0)
    cols[0] = ic

    def row_pass(r, carry):
        acc, hit = carry
        w = e[r] * cols[0, pl.ds(r, 1), :]
        z = jnp.where(hits(r, slice(None)), w, 0.0)
        for b in range(CH // 128):
            acc = acc + w[:, b * 128 : b * 128 + 128]
            hit = hit + z[:, b * 128 : b * 128 + 128]
        return acc, hit

    zero = jnp.zeros((Q, 128), f32)
    acc, hit = lax.fori_loop(0, NCH, row_pass, (zero, zero))
    parts = [
        jnp.sum(jnp.transpose(x[h * 128 : h * 128 + 128, :]), axis=0, keepdims=True)
        for x in (acc, hit)
        for h in range(2)
    ]
    rows[me] = jnp.concatenate(parts + [jnp.zeros((4, 128), f32)], axis=0)
    own_r = rows.at[me]

    def row_start(k, carry):
        j = k + k // (L - 4)
        to = hop(pos, j // 2) * 2 + (core + j) % 2
        remote(own_r, own_r, rw_s.at[k], rw_r.at[me], {"loop": to}).start()
        return carry

    def row_wait(k, carry):
        frm = (me + k) % L
        remote(own_r, rows.at[frm], rw_s.at[k - 1], rw_r.at[frm], {"loop": frm}).wait()
        return carry

    lax.fori_loop(0, L - 1, row_start, 0)
    lax.fori_loop(1, L, row_wait, 0)
    tot = jnp.sum(rows[...], axis=0)

    def spread(x):
        return jnp.transpose(jnp.broadcast_to(x, (128, 128)))

    inv = 1.0 / tot[0:2]
    for h in range(2):
        irc[h * 128 : h * 128 + 128, :] = spread(inv[h : h + 1])

    def grad_pass(r, carry):
        y = e[r] * wide(irc[...])
        cols2[grp, pl.ds(r, 1), :] = (
            jnp.sum(y, axis=0, keepdims=True) * cols[0, pl.ds(r, 1), :] - cnt[pl.ds(r, 1), :]
        )
        return carry

    lax.fori_loop(0, NCH, grad_pass, 0)
    finish = group_exchange(cols2, c2_s, c2_r)
    los = jnp.log(tot[0:2]) - jnp.log(tot[2:4])
    for h in range(2):
        zer = spread(los[h : h + 1])
        tmp[h * 128 : h * 128 + 128, :] = zer
    loss_ref[...] = tmp[pl.ds(pl.multiple_of(slot * N, N), N), :]
    finish()
    cols2[0] = jnp.sum(cols2[...], axis=0)

    def half_grad(c):
        rng = pl.ds(pl.multiple_of(c * 128, 128), 128)

        def chunk(r, carry):
            base = wide(irc[rng, :]) - cols2[0, pl.ds(r, 1), :]
            g = e[r, rng, :] * (cols[0, pl.ds(r, 1), :] * base)
            g = g - jnp.where(hits(r, rng), 1.0, 0.0)
            sgb[:, pl.ds(pl.multiple_of(r * CH, CH), CH)] = g.astype(bf16)
            return carry

        lax.fori_loop(0, NCH, chunk, 0)
        return SCALE * jnp.dot(sgb[...], u[...], preferred_element_type=f32)

    pacc[...] = half_grad(1 - core).reshape(H, N, D)
    to_mate = remote(pacc, prec, pp_s, pp_r, mate)
    to_mate.start()
    mine = half_grad(core).reshape(H, N, D)
    to_mate.wait()
    rsend[...] = mine + prec[...]

    def scatter_start(src, dst, send, recv):
        def start(k, carry):
            to = hop(pos, k + k // (H - 2))
            remote(src.at[to], dst.at[pos], send.at[k], recv.at[pos], peer(to)).start()
            return carry

        lax.fori_loop(0, H - 1, start, 0)

    def scatter_wait(src, dst, send, recv):
        def arrive(k, carry):
            frm = (pos + k) % H
            remote(src.at[frm], dst.at[frm], send.at[k - 1], recv.at[frm], peer(frm)).wait()
            return carry

        lax.fori_loop(1, H, arrive, 0)

    rrec[pos] = rsend[pos]
    scatter_start(rsend, rrec, rs_s, rs_r)
    scatter_wait(rsend, rrec, rs_s, rs_r)
    qg = jnp.sum(rrec[...], axis=0)

    eg = ((qg - unit * jnp.sum(unit * qg, axis=1, keepdims=True)) * inv_norm).astype(bf16)
    pg = lax.dot_general(eg, proj[...], (((1,), (1,)), ((), ())), preferred_element_type=f32)
    og = pg * (1.0 / PIX)
    centred = og - jnp.sum(og, axis=1, keepdims=True) * (1.0 / C)
    for t in range(T):
        xs[t] = og[:, t * 128 : t * 128 + 128]
        dkr[t, 0:N, :] = centred[:, t * 128 : t * 128 + 128]

    def hidden_row(i, carry):
        for j in range(S):
            p = i * S + j
            nrm = nf[:, p]
            m2 = jnp.sum(jnp.sum(nrm * xs[...], axis=0), axis=1, keepdims=True) * (1.0 / C)
            nf[:, p] = rsb[p][None] * (dkr[:, 0:N, :] - nrm * m2[None])
        return carry

    lax.fori_loop(0, S, hidden_row, 0)

    def kernel_tile(t, carry):
        dkr[t, 48:64, :] = jnp.zeros((16, 128), f32)
        for a in range(S):
            acc = [None] * S
            for i in range(S):
                r = i + a - 3
                if not 0 <= r < S:
                    continue
                x = [xf[t, r * S + c] for c in range(S)]
                g = [nf[t, i * S + c] for c in range(S)]
                for b in range(S):
                    for j in range(S):
                        c = j + b - 3
                        if 0 <= c < S:
                            term = x[c] * g[j]
                            acc[b] = term if acc[b] is None else acc[b] + term
            for b in range(S):
                dkr[t, a * S + b : a * S + b + 1, :] = jnp.sum(acc[b], axis=0, keepdims=True)
        flat = jnp.concatenate([dkr[t], jnp.zeros((64, 128), f32)], axis=0)
        kgt[lanes(t), :] = jnp.transpose(flat)
        return carry

    lax.fori_loop(0, T, kernel_tile, 0)

    def pack(l, carry):
        c = l % 2
        low = kgt[pl.ds(pl.multiple_of(l * 48, 8), 24), :]
        high = kgt[pl.ds(pl.multiple_of(l * 48 + 24, 8), 24), :]
        kps[c * H + l // 2] = low + pltpu.roll(high, 64, 1)
        return carry

    lax.fori_loop(0, L, pack, 0)
    other = pl.ds((1 - core) * H, H)
    k_mate = remote(kps.at[other], kprec, kp_s, kp_r, mate)
    k_mate.start()

    def image_tile(t, carry):
        for i, acc in conv_rows(
            lambda r, x: nf[t, r * S + x],
            lambda a, b: jnp.broadcast_to(kf[t, a * 8 + b : a * 8 + b + 1, :], (N, 128)),
            True,
        ):
            for j in range(S):
                tmp[pl.ds(i * 8 + j, N, stride=56), :] = acc[j] + xs[t]
        for n in range(N):
            for i in range(S):
                ig_ref[n, i, :, lanes(t)] = tmp[n * 56 + i * 8 : n * 56 + i * 8 + S, :].astype(bf16)
        return carry

    lax.fori_loop(0, 3, image_tile, 0)
    k_mate.wait()
    ksum = kps.at[pl.ds(core * H, H)]
    kprec[...] = kprec[...] + ksum[...]
    krec[pos] = kprec[pos]
    scatter_start(kprec, krec, ks_s, ks_r)
    lax.fori_loop(3, T, image_tile, 0)
    scatter_wait(kprec, krec, ks_s, ks_r)
    krec2[grp] = jnp.sum(krec[...], axis=0)
    group_exchange(krec2, k2_s, k2_r)()
    kg_ref[...] = jnp.sum(krec2[...], axis=0)


def shards(images, targets, kernel, projection, captions):
    vmem = pltpu.VMEM
    dma = pltpu.SemaphoreType.DMA
    anyspace = pl.BlockSpec(memory_space=pl.ANY)
    whole = pl.BlockSpec(memory_space=vmem)
    scratch = [
        vmem((N, S, S, C), bf16),
        vmem((C, D), bf16),
        vmem((CAPS, D), bf16),
        vmem((T, PIX, N, 128), f32),
        vmem((T, 56, 128), f32),
        vmem((N * 56, 128), f32),
        vmem((T, PIX, N, 128), f32),
        vmem((PIX, N, 128), f32),
        vmem((T, N, 128), f32),
        vmem((L, N, D), bf16),
        vmem((Q, D), bf16),
        vmem((Q, 128), f32),
        vmem((N, CH), f32),
        vmem((NCH, CH), f32),
        vmem((NCH, Q, CH), f32),
        vmem((Q, 128), f32),
        vmem((Q // 2, CAPS), bf16),
        vmem((G, NCH, CH), f32),
        vmem((G, NCH, CH), f32),
        vmem((L, 8, 128), f32),
        vmem((H, N, D), f32),
        vmem((H, N, D), f32),
        vmem((H, N, D), f32),
        vmem((H, N, D), f32),
        vmem((T, 64, 128), f32),
        vmem((C, 128), f32),
        vmem((L, 24, 128), f32),
        vmem((H, 24, 128), f32),
        vmem((H, 24, 128), f32),
        vmem((G, 24, 128), f32),
        dma((3,)), dma((H,)), dma((L,)), dma((H,)),
        dma((G,)), dma((G,)), dma((G,)), dma((G,)),
        dma((L,)), dma((L,)),
        dma, dma, dma((H,)), dma((H,)),
        dma, dma, dma((H,)), dma((H,)), dma((G,)), dma((G,)),
    ]
    loss, image_grad, kg = pl.pallas_call(
        mega,
        name="mega",
        out_shape=(
            jax.ShapeDtypeStruct((N, 128), f32),
            jax.ShapeDtypeStruct((N, S, S, C), bf16),
            jax.ShapeDtypeStruct((24, 128), f32),
        ),
        in_specs=[anyspace, whole, whole, anyspace, anyspace],
        out_specs=(whole, whole, whole),
        scratch_shapes=scratch,
        compiler_params=pltpu.CompilerParams(
            collective_id=0, has_side_effects=True, vmem_limit_bytes=60 * 1024 * 1024
        ),
    )(images[0], targets, kernel, projection, captions)
    own = jnp.concatenate([kg[:, 0:PIX], kg[:, 64 : 64 + PIX]], axis=0)
    kernel_share = lax.dynamic_slice_in_dim(own, lax.axis_index("group") * 6, 6, 0)
    return loss[:, 0][None], image_grad[None], kernel_share


def solution(mesh):
    placed = (P("group", "loop", None, None, None), P("group", None), P(), P(), P("loop", None))
    return jax.shard_map(
        shards,
        mesh=mesh,
        in_specs=placed,
        out_specs=(
            P("group", "loop"),
            P("group", "loop", None, None, None),
            P(("loop", "group"), None),
        ),
        check_vma=False,
    )
```

time: 740 us -> 97.3 us (0.13)
  waiting for transfers between devices: 380 us -> 0 us
  blocking collectives: 224 us -> 0 us
  other arithmetic: 98.7 us -> 0.61 us
  Pallas kernels: 0 us -> 88.9 us
  matrix products: 14.1 us -> 0 us
  between operations: 14.6 us -> 0.65 us
    unnamed x3 -> x0, waiting for transfers between devices: 212 us -> none
    psum x4 -> x0, blocking collectives: 184 us -> none  [the longest x2 120 us: shards(): row_sum, target_logit = lax.psum((row_part, target_part), 'loop')]
    psum x1 -> x0, waiting for transfers between devices: 168 us -> none  [shards(): summed = lax.psum(incomplete_gradient, 'loop')]
    pallas_call x0 -> x1, Pallas kernels: none -> 88.9 us  [shards(): pl.pallas_call(mega, name='mega', out_shape=(jax.ShapeDtypeStruct((N, 128...]
    reduce_sum x11 -> x0, other arithmetic: 56.2 us -> none  [the longest x1 31.9 us: forward(): centre = hidden - jnp.mean(hidden, -1, keepdims=True)]
    all_gather x1 -> x0, blocking collectives: 39.6 us -> none  [shards(): lax.all_gather(query, 'loop', axis=0, tiled=True)]
    broadcast_in_dim x1 -> x0, other arithmetic: 38 us -> none  [shards(): return (own_loss[None], input_grad.astype(jnp.bfloat16)[None], kernel_share)]
    dot_general x4 -> x0, matrix products: 14.1 us -> none  [the longest x1 8.03 us: shards(): jnp.dot(similarity_gradient, normalized_caption_vectors, preferred_elemen...]
  transfers between devices with their start and end apart: 2 -> 0, of which waited for: 2 -> 0; matrix products, arithmetic and copies ran while one was open for 5% -> 0% of each run, Pallas kernels for 0% -> 0%
where the time goes in v1:
time: 97.3 us; the launch traced here: 97.1 us
  Pallas kernels  88.9 us (91%)
  local copies, waits for them, and re-layouts  6.94 us (7%)
    pallas_call x1, Pallas kernels, shards(): pl.pallas_call(mega, name='mega', out_shape=(jax.ShapeDtypeStruct((N, 128...  88.9 us
    unnamed x4, local copies, waits for them, and re-layouts  5.56 us

profile of v1, /device:TPU:1, one launch (start us, length us, event | category | flops | bytes accessed | tf_op | source)
XLA Modules:
  0.0 97.1 jit_solution(8263051410426237181)
XLA Ops:
  0.6 2.8 %copy.13 = bf16[1,8,7,7,1536]{4,3,2,1,0:T(8,128)(2,1)} copy(bf16[1,8,7,7,1536]{4,1,3,2,0:T(8,128)(2,1)} %param.5) | data formatting | bytes 2408448 | tf_op args[0]
  3.4 88.9 %mega.1 = (f32[8,128]{1,0:T(8,128)}, bf16[8,7,7,1536]{3,2,1,0:T(8,128)(2,1)}, f32[24,128]{1,0:T(8,128)}) custom-call(bf16[8,7,7,1536]{3,2,1,0:T(8,128)(2,1)} %bitcast.5, s32[1,256]{1,0:T(1,128)} %tgt_ref.1, bf16[7,7,1536]{2,1,0:T(8,128)(2,1)} %ker_ref.1, bf16[1536,768]{1,0:T(8,128)(2,1)} %proj_hbm.1, bf16[4096,768]{1,0:T(8,128)(2,1)} %cap_hbm.1), custom_call_target="tpu_custom_call" | custom-call | tf_op jit(solution)/shard_map/mega/pallas_call | solution.py:466
  92.3 0.0 copy-start
  92.3 1.3 %slice_reduce_fusion = f32[8]{0:T(128)} fusion(f32[8,128]{1,0:T(8,128)} %get-tuple-element.6), kind=kLoop, calls=%fused_computation.4 | loop fusion | bytes 64 | tf_op jit(solution)/shard_map/slice | solution.py:483
  93.6 2.8 %copy.11 = bf16[1,8,7,7,1536]{4,1,3,2,0:T(8,128)(2,1)} copy(bf16[1,8,7,7,1536]{4,3,2,1,0:T(8,128)(2,1)} %bitcast.6) | data formatting | bytes 2408448
  96.4 0.0 copy-done
  96.4 0.1 fusion.1
  96.5 0.6 fusion
Async XLA Ops:
  92.3 4.1 %copy-start = (f32[24,128]{1,0:T(8,128)S(1)}, f32[24,128]{1,0:T(8,128)}, u32[]{:S(2)}) copy-start(f32[24,128]{1,0:T(8,128)} %get-tuple-element.8) | copy-start | bytes 36868

commit v2 on v1

--- a/solution.py
+++ b/solution.py
@@ -6,6 +6,7 @@
 from jax.sharding import PartitionSpec as P
 
 MESH = pl.DeviceIdType.MESH
+ORDER = (4, 5, 3, 6, 2, 7, 1, 0)
 f32, bf16 = jnp.float32, jnp.bfloat16
 
 SCALE = 20.0
@@ -26,13 +27,6 @@
     return pltpu.make_async_remote_copy(
         src_ref=src, dst_ref=dst, send_sem=send, recv_sem=recv, device_id=where, device_id_type=MESH
     )
-
-
-def hop(pos, k):
-    step, low = k // 2, k % 2
-    half = (step + 1) // 2
-    z = (pos // 2 + 4 + half * (2 * (step % 2) - 1)) % 8
-    return z * 2 + (pos + low) % 2
 
 
 def conv_rows(load, tap, flip):
@@ -56,9 +50,9 @@
 def mega(
     img_hbm, tgt_ref, ker_ref, proj_hbm, cap_hbm,
     loss_ref, ig_ref, kg_ref,
-    img, proj, u, xf, kf, tmp, nf, rsb, xs,
-    qslots, qb, tcol, iot, cnt, e, irc, sgb, cols, cols2, rows,
-    pacc, prec, rsend, rrec, dkr, kgt, kps, kprec, krec, krec2,
+    img, proj, u, xf, kf, mub, nf, rsb, xs,
+    qslots, qb, tcol, iot, cnt, e, irc, hit, pick, sgb, cols, cols2, rows,
+    pacc, prec, rsend, rrec, dkr, kgt, kps, kprec, ksend, krec, krec2,
     in_sem, ag_s, ag_r, fw_s, c1_s, c1_r, c2_s, c2_r, rw_s, rw_r,
     pp_s, pp_r, rs_s, rs_r, kp_s, kp_r, ks_s, ks_r, k2_s, k2_r,
 ):
@@ -80,11 +74,11 @@
     barrier = pltpu.get_barrier_semaphore()
 
     def greet_loop(k, carry):
-        pl.semaphore_signal(barrier, inc=1, device_id={"loop": (me + k) % L}, device_id_type=MESH)
+        pl.semaphore_signal(barrier, inc=1, device_id={"loop": lax.rem(me + k, L)}, device_id_type=MESH)
         return carry
 
     def greet_group(k, carry):
-        pl.semaphore_signal(barrier, inc=1, device_id={"group": (grp + k) % G}, device_id_type=MESH)
+        pl.semaphore_signal(barrier, inc=1, device_id={"group": lax.rem(grp + k, G)}, device_id_type=MESH)
         return carry
 
     lax.fori_loop(1, L, greet_loop, 0)
@@ -96,17 +90,13 @@
     c_img.wait()
 
     def forward_tile(t, carry):
-        for n in range(N):
-            for i in range(S):
-                tmp[n * 56 + i * 8 : n * 56 + i * 8 + S, :] = img[n, i, :, lanes(t)].astype(f32)
         for a in range(S):
             kf[t, a * 8 : a * 8 + S, :] = ker_ref[a, :, lanes(t)].astype(f32)
         total = None
-        for i in range(S):
-            for j in range(S):
-                v = tmp[pl.ds(i * 8 + j, N, stride=56), :]
-                xf[t, i * S + j] = v
-                total = v if total is None else total + v
+        for p in range(PIX):
+            v = img[p, :, lanes(t)].astype(f32)
+            xf[t, p] = v
+            total = v if total is None else total + v
         xs[t] = total
         for i, acc in conv_rows(
             lambda r, x: xf[t, r * S + x],
@@ -119,20 +109,31 @@
 
     lax.fori_loop(0, T, forward_tile, 0)
 
+    def lane_mean(x):
+        return jnp.broadcast_to(jnp.sum(x, axis=1, keepdims=True) * (1.0 / C), (N, 128))
+
+    def mean_row(i, carry):
+        for j in range(S):
+            mub[i * S + j] = lane_mean(jnp.sum(nf[:, i * S + j], axis=0))
+        return carry
+
+    def var_row(i, carry):
+        for j in range(S):
+            p = i * S + j
+            cen = nf[:, p] - mub[p][None]
+            rsb[p] = lax.rsqrt(lane_mean(jnp.sum(cen * cen, axis=0)) + EPS)
+        return carry
+
     def norm_row(i, acc):
         for j in range(S):
             p = i * S + j
-            h = nf[:, p]
-            mu = jnp.sum(jnp.sum(h, axis=0), axis=1, keepdims=True) * (1.0 / C)
-            cen = h - mu[None]
-            var = jnp.sum(jnp.sum(cen * cen, axis=0), axis=1, keepdims=True) * (1.0 / C)
-            rs = lax.rsqrt(var + EPS)
-            rsb[p] = jnp.broadcast_to(rs, (N, 128))
-            nrm = cen * rs[None]
+            nrm = (nf[:, p] - mub[p][None]) * rsb[p][None]
             nf[:, p] = nrm
             acc = acc + nrm
         return acc
 
+    lax.fori_loop(0, S, mean_row, 0)
+    lax.fori_loop(0, S, var_row, 0)
     nsum = lax.fori_loop(0, S, norm_row, xs[...])
     pooled = (nsum * (1.0 / PIX)).astype(bf16)
     pooled = jnp.concatenate([pooled[t] for t in range(T)], axis=1)
@@ -145,12 +146,12 @@
     pl.semaphore_wait(barrier, L - 1 + G - 1)
     own_q = qslots.at[slot]
 
-    def ag_send(k, carry):
-        to = hop(pos, k + k // (H - 2))
-        remote(own_q, own_q, ag_s.at[k], ag_r.at[slot], peer(to)).start()
-        return carry
-
-    lax.fori_loop(0, H - 1, ag_send, 0)
+    def around(start):
+        for k in range(H - 1):
+            j = k + k // (H - 2)
+            start(k, lax.rem(pos // 2 + ORDER[j // 2], 8) * 2 + lax.rem(pos % 2 + j % 2, 2))
+
+    around(lambda k, to: remote(own_q, own_q, ag_s.at[k], ag_r.at[slot], peer(to)).start())
     remote(own_q, own_q, fw_s.at[0], ag_r.at[slot], mate).start()
 
     c_cap.wait()
@@ -175,17 +176,16 @@
         return jnp.concatenate([x] * (CH // 128), axis=1)
 
     def hits(r, rng):
-        ids = iot[0:1, :] + (r * CH).astype(f32)
+        ids = iot[0:1, :] + (r * float(CH) if isinstance(r, int) else (r * CH).astype(f32))
         return wide(tcol[rng, :]) == ids
 
     def count(r, carry):
         cnt[pl.ds(r, 1), :] = jnp.sum(jnp.where(hits(r, slice(None)), 1.0, 0.0), axis=0, keepdims=True)
         return carry
 
-    lax.fori_loop(0, NCH, count, 0)
 
     def ag_forward(k, carry):
-        frm = core * H + (pos + k) % H
+        frm = core * H + lax.rem(pos + k, H)
         got = qslots.at[frm]
         remote(got, got, ag_s.at[0], ag_r.at[frm], mate).wait_recv()
         remote(got, got, fw_s.at[k], ag_r.at[frm], mate).start()
@@ -227,59 +227,88 @@
         own = buf.at[grp]
 
         def start(k, carry):
-            remote(own, own, send.at[k], recv.at[grp], {"group": (grp + k) % G}).start()
+            remote(own, own, send.at[k], recv.at[grp], {"group": lax.rem(grp + k, G)}).start()
             return carry
 
         def arrive(k, carry):
-            frm = (grp + k) % G
+            frm = lax.rem(grp + k, G)
             remote(own, buf.at[frm], send.at[k], recv.at[frm], {"group": frm}).wait()
             return carry
 
         lax.fori_loop(1, G, start, 0)
         return lambda: lax.fori_loop(1, G, arrive, 0)
 
-    group_exchange(cols, c1_s, c1_r)()
+    def picked(c, carry):
+        rng = pl.ds(pl.multiple_of(c * 128, 128), 128)
+
+        def chunk(r, carry):
+            sgb[:, pl.ds(pl.multiple_of(r * CH, CH), CH)] = jnp.where(hits(r, rng), 1.0, 0.0).astype(bf16)
+            return carry
+
+        lax.fori_loop(0, NCH, chunk, 0)
+        pick[c] = jnp.dot(sgb[...], u[...], preferred_element_type=f32)
+        return carry
+
+    finish = group_exchange(cols, c1_s, c1_r)
+    lax.fori_loop(0, NCH, count, 0)
+    lax.fori_loop(0, 2, picked, 0)
+    finish()
     ic = 1.0 / jnp.sum(cols[...], axis=0)
     cols[0] = ic
 
-    def row_pass(r, carry):
-        acc, hit = carry
-        w = e[r] * cols[0, pl.ds(r, 1), :]
-        z = jnp.where(hits(r, slice(None)), w, 0.0)
-        for b in range(CH // 128):
-            acc = acc + w[:, b * 128 : b * 128 + 128]
-            hit = hit + z[:, b * 128 : b * 128 + 128]
-        return acc, hit
-
-    zero = jnp.zeros((Q, 128), f32)
-    acc, hit = lax.fori_loop(0, NCH, row_pass, (zero, zero))
-    parts = [
-        jnp.sum(jnp.transpose(x[h * 128 : h * 128 + 128, :]), axis=0, keepdims=True)
-        for x in (acc, hit)
-        for h in range(2)
-    ]
-    rows[me] = jnp.concatenate(parts + [jnp.zeros((4, 128), f32)], axis=0)
+    def row_pass(q, carry):
+        rng = pl.ds(pl.multiple_of(q * 32, 32), 32)
+        acc = None
+        for r in range(NCH):
+            w = e[r, rng, :] * cols[0, r : r + 1, :]
+            for b in range(CH // 128):
+                v = w[:, b * 128 : b * 128 + 128]
+                acc = v if acc is None else acc + v
+        irc[rng, :] = acc
+        return carry
+
+    lax.fori_loop(0, Q // 32, row_pass, 0)
+    rows[me] = jnp.concatenate(
+        [jnp.sum(jnp.transpose(irc[h * 128 : h * 128 + 128, :]), axis=0, keepdims=True) for h in range(2)], axis=0
+    )
     own_r = rows.at[me]
 
-    def row_start(k, carry):
-        j = k + k // (L - 4)
-        to = hop(pos, j // 2) * 2 + (core + j) % 2
+    for k in range(L):
+        zo, low = ORDER[k // 4], k % 4
+        if zo == 0 and low == 0:
+            continue
+        to = (lax.rem(pos // 2 + zo, 8) * 2 + lax.rem(pos % 2 + low // 2, 2)) * 2 + lax.rem(core + low % 2, 2)
         remote(own_r, own_r, rw_s.at[k], rw_r.at[me], {"loop": to}).start()
-        return carry
+
+    def hit_pass(q, carry):
+        rng = pl.ds(pl.multiple_of(q * 32, 32), 32)
+        acc = None
+        for r in range(NCH):
+            z = jnp.where(hits(r, rng), e[r, rng, :] * cols[0, r : r + 1, :], 0.0)
+            for b in range(CH // 128):
+                v = z[:, b * 128 : b * 128 + 128]
+                acc = v if acc is None else acc + v
+        hit[rng, :] = acc
+        return carry
+
+    lax.fori_loop(0, Q // 32, hit_pass, 0)
 
     def row_wait(k, carry):
-        frm = (me + k) % L
-        remote(own_r, rows.at[frm], rw_s.at[k - 1], rw_r.at[frm], {"loop": frm}).wait()
-        return carry
-
-    lax.fori_loop(0, L - 1, row_start, 0)
+        frm = lax.rem(me + k, L)
+        remote(own_r, rows.at[frm], rw_s.at[0], rw_r.at[frm], {"loop": frm}).wait_recv()
+        return carry
+
+    def row_sent(k, carry):
+        remote(own_r, own_r, rw_s.at[k], rw_r.at[0], mate).wait_send()
+        return carry
+
     lax.fori_loop(1, L, row_wait, 0)
     tot = jnp.sum(rows[...], axis=0)
 
     def spread(x):
         return jnp.transpose(jnp.broadcast_to(x, (128, 128)))
 
-    inv = 1.0 / tot[0:2]
+    inv = 1.0 / tot
     for h in range(2):
         irc[h * 128 : h * 128 + 128, :] = spread(inv[h : h + 1])
 
@@ -292,11 +321,9 @@
 
     lax.fori_loop(0, NCH, grad_pass, 0)
     finish = group_exchange(cols2, c2_s, c2_r)
-    los = jnp.log(tot[0:2]) - jnp.log(tot[2:4])
-    for h in range(2):
-        zer = spread(los[h : h + 1])
-        tmp[h * 128 : h * 128 + 128, :] = zer
-    loss_ref[...] = tmp[pl.ds(pl.multiple_of(slot * N, N), N), :]
+    for k in range(L):
+        if k != ORDER.index(0) * 4:
+            row_sent(k, 0)
     finish()
     cols2[0] = jnp.sum(cols2[...], axis=0)
 
@@ -306,31 +333,36 @@
         def chunk(r, carry):
             base = wide(irc[rng, :]) - cols2[0, pl.ds(r, 1), :]
             g = e[r, rng, :] * (cols[0, pl.ds(r, 1), :] * base)
-            g = g - jnp.where(hits(r, rng), 1.0, 0.0)
             sgb[:, pl.ds(pl.multiple_of(r * CH, CH), CH)] = g.astype(bf16)
             return carry
 
         lax.fori_loop(0, NCH, chunk, 0)
-        return SCALE * jnp.dot(sgb[...], u[...], preferred_element_type=f32)
-
-    pacc[...] = half_grad(1 - core).reshape(H, N, D)
+        return SCALE * (jnp.dot(sgb[...], u[...], preferred_element_type=f32) - pick[c])
+
+    def with_hits(c):
+        part = hit[pl.ds(pl.multiple_of(c * 128, 128), 128), :]
+        return jnp.concatenate([half_grad(c), part], axis=1).reshape(H, N, D + 128)
+
+    pacc[...] = with_hits(1 - core)
     to_mate = remote(pacc, prec, pp_s, pp_r, mate)
     to_mate.start()
-    mine = half_grad(core).reshape(H, N, D)
+    mine = with_hits(core)
     to_mate.wait()
-    rsend[...] = mine + prec[...]
+    both = (mine + prec[...]).reshape(H * N, D + 128)
+    found = jnp.broadcast_to(jnp.sum(both[:, D:], axis=1, keepdims=True), (H * N, 128))
+    first = found.astype(bf16).astype(f32)
+    second = (found - first).astype(bf16).astype(f32)
+    lane = lax.broadcasted_iota(jnp.int32, (H * N, 128), 1)
+    found = jnp.where(lane == 0, first, jnp.where(lane == 1, second, jnp.where(lane == 2, found - first - second, 0.0)))
+    both = jnp.concatenate([both[:, 0:D], found], axis=1).reshape(H, N, D + 128)
+    rsend[...] = both.astype(bf16)
 
     def scatter_start(src, dst, send, recv):
-        def start(k, carry):
-            to = hop(pos, k + k // (H - 2))
-            remote(src.at[to], dst.at[pos], send.at[k], recv.at[pos], peer(to)).start()
-            return carry
-
-        lax.fori_loop(0, H - 1, start, 0)
+        around(lambda k, to: remote(src.at[to], dst.at[pos], send.at[k], recv.at[pos], peer(to)).start())
 
     def scatter_wait(src, dst, send, recv):
         def arrive(k, carry):
-            frm = (pos + k) % H
+            frm = lax.rem(pos + k, H)
             remote(src.at[frm], dst.at[frm], send.at[k - 1], recv.at[frm], peer(frm)).wait()
             return carry
 
@@ -339,7 +371,10 @@
     rrec[pos] = rsend[pos]
     scatter_start(rsend, rrec, rs_s, rs_r)
     scatter_wait(rsend, rrec, rs_s, rs_r)
-    qg = jnp.sum(rrec[...], axis=0)
+    qh = jnp.sum(rrec[...].astype(f32), axis=0)
+    qg = qh[:, 0:D]
+    own_rows = irc[pl.ds(pl.multiple_of(slot * N, N), N), :]
+    loss_ref[...] = -jnp.log(own_rows) - jnp.log(jnp.sum(qh[:, D:], axis=1, keepdims=True))
 
     eg = ((qg - unit * jnp.sum(unit * qg, axis=1, keepdims=True)) * inv_norm).astype(bf16)
     pg = lax.dot_general(eg, proj[...], (((1,), (1,)), ((), ())), preferred_element_type=f32)
@@ -402,22 +437,21 @@
             True,
         ):
             for j in range(S):
-                tmp[pl.ds(i * 8 + j, N, stride=56), :] = acc[j] + xs[t]
-        for n in range(N):
-            for i in range(S):
-                ig_ref[n, i, :, lanes(t)] = tmp[n * 56 + i * 8 : n * 56 + i * 8 + S, :].astype(bf16)
+                ig_ref[i * S + j, :, lanes(t)] = (acc[j] + xs[t]).astype(bf16)
         return carry
 
     lax.fori_loop(0, 3, image_tile, 0)
     k_mate.wait()
     ksum = kps.at[pl.ds(core * H, H)]
-    kprec[...] = kprec[...] + ksum[...]
-    krec[pos] = kprec[pos]
-    scatter_start(kprec, krec, ks_s, ks_r)
-    lax.fori_loop(3, T, image_tile, 0)
-    scatter_wait(kprec, krec, ks_s, ks_r)
-    krec2[grp] = jnp.sum(krec[...], axis=0)
-    group_exchange(krec2, k2_s, k2_r)()
+    ksend[...] = (kprec[...] + ksum[...]).astype(bf16)
+    krec[pos] = ksend[pos]
+    scatter_start(ksend, krec, ks_s, ks_r)
+    lax.fori_loop(3, 9, image_tile, 0)
+    scatter_wait(ksend, krec, ks_s, ks_r)
+    krec2[grp] = jnp.sum(krec[...].astype(f32), axis=0)
+    finish = group_exchange(krec2, k2_s, k2_r)
+    lax.fori_loop(9, T, image_tile, 0)
+    finish()
     kg_ref[...] = jnp.sum(krec2[...], axis=0)
 
 
@@ -427,12 +461,12 @@
     anyspace = pl.BlockSpec(memory_space=pl.ANY)
     whole = pl.BlockSpec(memory_space=vmem)
     scratch = [
-        vmem((N, S, S, C), bf16),
+        vmem((PIX, N, C), bf16),
         vmem((C, D), bf16),
         vmem((CAPS, D), bf16),
         vmem((T, PIX, N, 128), f32),
         vmem((T, 56, 128), f32),
-        vmem((N * 56, 128), f32),
+        vmem((PIX, N, 128), f32),
         vmem((T, PIX, N, 128), f32),
         vmem((PIX, N, 128), f32),
         vmem((T, N, 128), f32),
@@ -443,19 +477,22 @@
         vmem((NCH, CH), f32),
         vmem((NCH, Q, CH), f32),
         vmem((Q, 128), f32),
+        vmem((Q, 128), f32),
+        vmem((2, Q // 2, D), f32),
         vmem((Q // 2, CAPS), bf16),
         vmem((G, NCH, CH), f32),
         vmem((G, NCH, CH), f32),
-        vmem((L, 8, 128), f32),
-        vmem((H, N, D), f32),
-        vmem((H, N, D), f32),
-        vmem((H, N, D), f32),
-        vmem((H, N, D), f32),
+        vmem((L, 2, 128), f32),
+        vmem((H, N, D + 128), f32),
+        vmem((H, N, D + 128), f32),
+        vmem((H, N, D + 128), bf16),
+        vmem((H, N, D + 128), bf16),
         vmem((T, 64, 128), f32),
         vmem((C, 128), f32),
         vmem((L, 24, 128), f32),
         vmem((H, 24, 128), f32),
-        vmem((H, 24, 128), f32),
+        vmem((H, 24, 128), bf16),
+        vmem((H, 24, 128), bf16),
         vmem((G, 24, 128), f32),
         dma((3,)), dma((H,)), dma((L,)), dma((H,)),
         dma((G,)), dma((G,)), dma((G,)), dma((G,)),
@@ -468,7 +505,7 @@
         name="mega",
         out_shape=(
             jax.ShapeDtypeStruct((N, 128), f32),
-            jax.ShapeDtypeStruct((N, S, S, C), bf16),
+            jax.ShapeDtypeStruct((PIX, N, C), bf16),
             jax.ShapeDtypeStruct((24, 128), f32),
         ),
         in_specs=[anyspace, whole, whole, anyspace, anyspace],
@@ -477,9 +514,10 @@
         compiler_params=pltpu.CompilerParams(
             collective_id=0, has_side_effects=True, vmem_limit_bytes=60 * 1024 * 1024
         ),
-    )(images[0], targets, kernel, projection, captions)
+    )(jnp.transpose(images[0], (1, 2, 0, 3)).reshape(PIX, N, C), targets, kernel, projection, captions)
     own = jnp.concatenate([kg[:, 0:PIX], kg[:, 64 : 64 + PIX]], axis=0)
     kernel_share = lax.dynamic_slice_in_dim(own, lax.axis_index("group") * 6, 6, 0)
+    image_grad = jnp.transpose(image_grad.reshape(S, S, N, C), (2, 0, 1, 3))
     return loss[:, 0][None], image_grad[None], kernel_share
 
 

time: 97.3 us -> 85.7 us (0.88)
  Pallas kernels: 88.9 us -> 79.7 us
  local copies, waits for them, and re-layouts: 6.94 us -> 4.54 us
    pallas_call x1, Pallas kernels: 88.9 us -> 79.7 us  [shards(): pl.pallas_call(mega, name='mega', out_shape=(jax.ShapeDtypeStruct((N, 128...]
    unnamed x4 -> x1, local copies, waits for them, and re-layouts: 5.56 us -> 2.38 us
where the time goes in v2:
time: 85.7 us; the launch traced here: 85.4 us
  Pallas kernels  79.7 us (93%)
  local copies, waits for them, and re-layouts  4.54 us (5%)
    pallas_call x1, Pallas kernels, shards(): pl.pallas_call(mega, name='mega', out_shape=(jax.ShapeDtypeStruct((N, 128...  79.7 us
    unnamed x1, local copies, waits for them, and re-layouts  2.38 us

profile of v2, /device:TPU:1, one launch (start us, length us, event | category | flops | bytes accessed | tf_op | source)
XLA Modules:
  0.0 85.4 jit_solution(11294941296625726026)
XLA Ops:
  0.6 79.7 %mega.1 = (f32[8,128]{1,0:T(8,128)}, bf16[49,8,1536]{2,1,0:T(8,128)(2,1)}, f32[24,128]{1,0:T(8,128)}) custom-call(bf16[49,8,1536]{2,1,0:T(8,128)(2,1)} %bitcast.12, s32[1,256]{1,0:T(1,128)} %tgt_ref.1, bf16[7,7,1536]{2,1,0:T(8,128)(2,1)} %ker_ref.1, bf16[1536,768]{1,0:T(8,128)(2,1)} %proj_hbm.1, bf16[4096,768]{1,0:T(8,128)(2,1)} %cap_hbm.1), custom_call_target="tpu_custom_call" | custom-call | tf_op jit(solution)/shard_map/mega/pallas_call | solution.py:503
  80.3 0.9 %fusion.1 = (f32[24,49]{1,0:T(8,128)S(1)}, f32[24,49]{1,0:T(8,128)S(1)}) fusion(f32[24,128]{1,0:T(8,128)} %get-tuple-element.8), kind=kLoop, calls=%fused_computation.4 | loop fusion | bytes 18816 | tf_op jit(solution)/shard_map/slice | solution.py:518
  81.1 0.6 fusion
  81.8 1.3 %slice_reduce_fusion = f32[8]{0:T(128)} fusion(f32[8,128]{1,0:T(8,128)} %get-tuple-element.6), kind=kLoop, calls=%fused_computation.3 | loop fusion | bytes 64 | tf_op jit(solution)/shard_map/slice | solution.py:521
  83.1 2.4 %copy.9 = bf16[1,8,7,7,1536]{4,1,3,2,0:T(8,128)(2,1)} copy(bf16[1,8,7,7,1536]{4,1,3,2,0:T(8,128)(2,1)} %bitcast.11) | data formatting | bytes 2408448

commit v3 on v2

--- a/solution.py
+++ b/solution.py
@@ -29,30 +29,47 @@
     )
 
 
-def conv_rows(load, tap, flip):
-    for i in range(S):
-        acc = [None] * S
-        for a in range(S):
-            r = i + a - 3
-            if not 0 <= r < S:
+PAIRS = ((4, 3), (2, 3), (6, 5), (4, 5), (2, 1), (0, 1))
+
+
+def macs(acc, row, tap):
+    for b in range(S):
+        w = tap(b)
+        for j in range(S):
+            if 0 <= j + b - 3 < S:
+                term = row[j + b - 3] * w
+                acc[j] = term if acc[j] is None else acc[j] + term
+
+
+def conv_rows(load, pair, tap, diff):
+    def row(r):
+        return [load(r, x) for x in range(S)]
+
+    for o in range(4):
+        both, low, high = [None] * S, [None] * S, [None] * S
+        for q in range(4):
+            d = q - o
+            if abs(d) <= 1 and o < 3 and q < 3:
+                a = 2 * d + 3
+                macs(both, [pair(q, x) for x in range(S)], lambda b: tap(a, b))
+                macs(low, row(2 * q + 1), lambda b: diff(a + 1, a, b))
+                macs(high, row(2 * q), lambda b: diff(a - 1, a, b))
                 continue
-            row = [load(r, x) for x in range(S)]
-            for b in range(S):
-                w = tap(S - 1 - a, S - 1 - b) if flip else tap(a, b)
-                for j in range(S):
-                    x = j + b - 3
-                    if 0 <= x < S:
-                        term = row[x] * w
-                        acc[j] = term if acc[j] is None else acc[j] + term
-        yield i, acc
+            for r in (2 * q, 2 * q + 1):
+                for i, acc in ((2 * o, low), (2 * o + 1, high)):
+                    if r < S and i < S and 0 <= r - i + 3 < S:
+                        macs(acc, row(r), lambda b: tap(r - i + 3, b))
+        for i, acc in ((2 * o, low), (2 * o + 1, high)):
+            if i < S:
+                yield i, [v if w is None else v + w for v, w in zip(acc, both)]
 
 
 def mega(
     img_hbm, tgt_ref, ker_ref, proj_hbm, cap_hbm,
     loss_ref, ig_ref, kg_ref,
-    img, proj, u, xf, kf, mub, nf, rsb, xs,
+    img, proj, u, xf, kf, mub, nf, rsb, xs, kd, prs,
     qslots, qb, tcol, iot, cnt, e, irc, hit, pick, sgb, cols, cols2, rows,
-    pacc, prec, rsend, rrec, dkr, kgt, kps, kprec, ksend, krec, krec2,
+    pacc, prec, rsend, rrec, dkr, kgt, kps, kprec, ksend, krec, krec2, kout,
     in_sem, ag_s, ag_r, fw_s, c1_s, c1_r, c2_s, c2_r, rw_s, rw_r,
     pp_s, pp_r, rs_s, rs_r, kp_s, kp_r, ks_s, ks_r, k2_s, k2_r,
 ):
@@ -88,6 +105,13 @@
         return pl.ds(pl.multiple_of(t * 128, 128), 128)
 
     c_img.wait()
+
+    def tap_of(t, a, b):
+        return jnp.broadcast_to(kf[t, a * 8 + b : a * 8 + b + 1, :], (N, 128))
+
+    def diff_of(t, hi, lo, b):
+        n = PAIRS.index((hi, lo)) * 8 + b
+        return jnp.broadcast_to(kd[t, n : n + 1, :], (N, 128))
 
     def forward_tile(t, carry):
         for a in range(S):
@@ -98,10 +122,16 @@
             xf[t, p] = v
             total = v if total is None else total + v
         xs[t] = total
+        for n, (hi, lo) in enumerate(PAIRS):
+            kd[t, n * 8 : n * 8 + 8, :] = kf[t, hi * 8 : hi * 8 + 8, :] - kf[t, lo * 8 : lo * 8 + 8, :]
+        for q in range(3):
+            for x in range(S):
+                prs[q * S + x] = xf[t, 2 * q * S + x] + xf[t, (2 * q + 1) * S + x]
         for i, acc in conv_rows(
             lambda r, x: xf[t, r * S + x],
-            lambda a, b: jnp.broadcast_to(kf[t, a * 8 + b : a * 8 + b + 1, :], (N, 128)),
-            False,
+            lambda q, x: prs[q * S + x],
+            lambda a, b: tap_of(t, a, b),
+            lambda hi, lo, b: diff_of(t, hi, lo, b),
         ):
             for j in range(S):
                 nf[t, i * S + j] = acc[j]
@@ -374,7 +404,9 @@
     qh = jnp.sum(rrec[...].astype(f32), axis=0)
     qg = qh[:, 0:D]
     own_rows = irc[pl.ds(pl.multiple_of(slot * N, N), N), :]
-    loss_ref[...] = -jnp.log(own_rows) - jnp.log(jnp.sum(qh[:, D:], axis=1, keepdims=True))
+    los = -jnp.log(own_rows) - jnp.log(jnp.sum(qh[:, D:], axis=1, keepdims=True))
+    eye = lax.broadcasted_iota(jnp.int32, (N, 128), 0) == lax.broadcasted_iota(jnp.int32, (N, 128), 1)
+    loss_ref[...] = jnp.sum(jnp.where(eye, los, 0.0), axis=0, keepdims=True)[:, 0:N]
 
     eg = ((qg - unit * jnp.sum(unit * qg, axis=1, keepdims=True)) * inv_norm).astype(bf16)
     pg = lax.dot_general(eg, proj[...], (((1,), (1,)), ((), ())), preferred_element_type=f32)
@@ -396,22 +428,45 @@
 
     def kernel_tile(t, carry):
         dkr[t, 48:64, :] = jnp.zeros((16, 128), f32)
+        def corr(acc, x, g):
+            for b in range(S):
+                for j in range(S):
+                    if 0 <= j + b - 3 < S:
+                        term = x[j + b - 3] * g[j]
+                        acc[b] = term if acc[b] is None else acc[b] + term
+
+        def line(ref, r):
+            return [ref[t, r * S + c] for c in range(S)]
+
+        def fold(a, acc, first):
+            for b in range(S):
+                v = jnp.sum(acc[b], axis=0, keepdims=True)
+                at = slice(a * S + b, a * S + b + 1)
+                dkr[t, at, :] = v if first else dkr[t, at, :] + v
+
         for a in range(S):
             acc = [None] * S
             for i in range(S):
                 r = i + a - 3
-                if not 0 <= r < S:
+                if 0 <= r < S and (r // 2 == 3 or i // 2 == 3 or abs(r // 2 - i // 2) > 1):
+                    corr(acc, line(xf, r), line(nf, i))
+            if acc[0] is None:
+                dkr[t, a * S : a * S + S, :] = jnp.zeros((S, 128), f32)
+            else:
+                fold(a, acc, True)
+        for d in (-1, 0, 1):
+            both, low, high = [None] * S, [None] * S, [None] * S
+            for o in range(3):
+                q = o + d
+                if not 0 <= q < 3:
                     continue
-                x = [xf[t, r * S + c] for c in range(S)]
-                g = [nf[t, i * S + c] for c in range(S)]
-                for b in range(S):
-                    for j in range(S):
-                        c = j + b - 3
-                        if 0 <= c < S:
-                            term = x[c] * g[j]
-                            acc[b] = term if acc[b] is None else acc[b] + term
-            for b in range(S):
-                dkr[t, a * S + b : a * S + b + 1, :] = jnp.sum(acc[b], axis=0, keepdims=True)
+                x0, x1, g0, g1 = line(xf, 2 * q), line(xf, 2 * q + 1), line(nf, 2 * o), line(nf, 2 * o + 1)
+                corr(low, x1, g0)
+                corr(high, x0, g1)
+                corr(both, [u0 + u1 for u0, u1 in zip(x0, x1)], [u0 + u1 for u0, u1 in zip(g0, g1)])
+            fold(2 * d + 3, [v - (l0 + h0) for v, l0, h0 in zip(both, low, high)], False)
+            fold(2 * d + 4, low, False)
+            fold(2 * d + 2, high, False)
         flat = jnp.concatenate([dkr[t], jnp.zeros((64, 128), f32)], axis=0)
         kgt[lanes(t), :] = jnp.transpose(flat)
         return carry
@@ -431,10 +486,14 @@
     k_mate.start()
 
     def image_tile(t, carry):
+        for q in range(3):
+            for x in range(S):
+                prs[q * S + x] = nf[t, 2 * q * S + x] + nf[t, (2 * q + 1) * S + x]
         for i, acc in conv_rows(
             lambda r, x: nf[t, r * S + x],
-            lambda a, b: jnp.broadcast_to(kf[t, a * 8 + b : a * 8 + b + 1, :], (N, 128)),
-            True,
+            lambda q, x: prs[q * S + x],
+            lambda a, b: tap_of(t, S - 1 - a, S - 1 - b),
+            lambda hi, lo, b: diff_of(t, S - 1 - hi, S - 1 - lo, S - 1 - b),
         ):
             for j in range(S):
                 ig_ref[i * S + j, :, lanes(t)] = (acc[j] + xs[t]).astype(bf16)
@@ -452,7 +511,10 @@
     finish = group_exchange(krec2, k2_s, k2_r)
     lax.fori_loop(9, T, image_tile, 0)
     finish()
-    kg_ref[...] = jnp.sum(krec2[...], axis=0)
+    kout[24:32, :] = jnp.zeros((8, 128), f32)
+    kout[0:24, :] = jnp.sum(krec2[...], axis=0)
+    quarter = kout[pl.ds(lax.rem(grp, 4) * 6, 8), :]
+    kg_ref[...] = pltpu.roll(quarter, lax.div(grp, 4) * 64, 1)[0:6, 0:PIX]
 
 
 def shards(images, targets, kernel, projection, captions):
@@ -470,6 +532,8 @@
         vmem((T, PIX, N, 128), f32),
         vmem((PIX, N, 128), f32),
         vmem((T, N, 128), f32),
+        vmem((T, 48, 128), f32),
+        vmem((21, N, 128), f32),
         vmem((L, N, D), bf16),
         vmem((Q, D), bf16),
         vmem((Q, 128), f32),
@@ -494,6 +558,7 @@
         vmem((H, 24, 128), bf16),
         vmem((H, 24, 128), bf16),
         vmem((G, 24, 128), f32),
+        vmem((32, 128), f32),
         dma((3,)), dma((H,)), dma((L,)), dma((H,)),
         dma((G,)), dma((G,)), dma((G,)), dma((G,)),
         dma((L,)), dma((L,)),
@@ -504,9 +569,9 @@
         mega,
         name="mega",
         out_shape=(
-            jax.ShapeDtypeStruct((N, 128), f32),
+            jax.ShapeDtypeStruct((1, N), f32),
             jax.ShapeDtypeStruct((PIX, N, C), bf16),
-            jax.ShapeDtypeStruct((24, 128), f32),
+            jax.ShapeDtypeStruct((6, PIX), f32),
         ),
         in_specs=[anyspace, whole, whole, anyspace, anyspace],
         out_specs=(whole, whole, whole),
@@ -515,10 +580,8 @@
             collective_id=0, has_side_effects=True, vmem_limit_bytes=60 * 1024 * 1024
         ),
     )(jnp.transpose(images[0], (1, 2, 0, 3)).reshape(PIX, N, C), targets, kernel, projection, captions)
-    own = jnp.concatenate([kg[:, 0:PIX], kg[:, 64 : 64 + PIX]], axis=0)
-    kernel_share = lax.dynamic_slice_in_dim(own, lax.axis_index("group") * 6, 6, 0)
     image_grad = jnp.transpose(image_grad.reshape(S, S, N, C), (2, 0, 1, 3))
-    return loss[:, 0][None], image_grad[None], kernel_share
+    return loss, image_grad[None], kg
 
 
 def solution(mesh):

time: 85.7 us -> 84.2 us (0.982)
    slice x2 -> x0, local copies, waits for them, and re-layouts: 2.16 us -> none  [the longest x1 1.3 us: shards(): return (loss[:, 0][None], image_grad[None], kernel_share)]
    unnamed x1 -> x5, local copies, waits for them, and re-layouts: 2.38 us -> 4.16 us
where the time goes in v3:
time: 84.2 us; the launch traced here: 83.9 us
  Pallas kernels  79.1 us (94%)
  local copies, waits for them, and re-layouts  4.16 us (5%)
    pallas_call x1, Pallas kernels, shards(): pl.pallas_call(mega, name='mega', out_shape=(jax.ShapeDtypeStruct((1, N),...  79.1 us
    unnamed x5, local copies, waits for them, and re-layouts  4.16 us

profile of v3, /device:TPU:1, one launch (start us, length us, event | category | flops | bytes accessed | tf_op | source)
XLA Modules:
  0.0 83.9 jit_solution(1922180153292509051)
XLA Ops:
  0.6 79.1 %mega.1 = (f32[1,8]{1,0:T(1,128)}, bf16[49,8,1536]{2,1,0:T(8,128)(2,1)}, f32[6,49]{1,0:T(8,128)}) custom-call(bf16[49,8,1536]{2,1,0:T(8,128)(2,1)} %bitcast.11, s32[1,256]{1,0:T(1,128)} %tgt_ref.1, bf16[7,7,1536]{2,1,0:T(8,128)(2,1)} %ker_ref.1, bf16[1536,768]{1,0:T(8,128)(2,1)} %proj_hbm.1, bf16[4096,768]{1,0:T(8,128)(2,1)} %cap_hbm.1), custom_call_target="tpu_custom_call" | custom-call | tf_op jit(solution)/shard_map/mega/pallas_call | solution.py:568
  79.8 1.2 %copy.11 = f32[1,8]{1,0:T(1,128)} copy(f32[1,8]{1,0:T(1,128)} %get-tuple-element.12) | data formatting | bytes 64
  81.0 0.0 copy-start
  81.0 2.4 %copy.12 = bf16[1,8,7,7,1536]{4,1,3,2,0:T(8,128)(2,1)} copy(bf16[1,8,7,7,1536]{4,1,3,2,0:T(8,128)(2,1)} %bitcast.10) | data formatting | bytes 2408448
  83.3 0.0 copy-done
  83.4 0.6 copy.13
Async XLA Ops:
  81.0 2.4 %copy-start = (f32[6,49]{1,0:T(8,128)S(1)}, f32[6,49]{1,0:T(8,128)}, u32[]{:S(2)}) copy-start(f32[6,49]{1,0:T(8,128)} %get-tuple-element.14) | copy-start | bytes 3532
